TPU v7x, 32 devices: a whole 2x2x4 slice. The times are simulated.
32 devices in a mesh: groups: 2 (over y), seq: 4 (over z), fsdp: 2 (over x), head: 2 (over core).
Axes of the slice: x: 2, y: 2, z: 4, core: 2. Of those that a mesh axis runs over, the one named last changes fastest.
Arguments:
- frames: bfloat16 [6144, 3072], P(('groups', 'seq')), parts along dimension 0, may hold values from -330 to 330
- modulation: float32 [4, 3072], P('groups'), parts along dimension 0, may hold values from -2.5 to 2.5
- w_qkv: bfloat16 [3072, 3, 2048], P('seq', None, ('fsdp', 'head')), may hold values from -0.109375 to 0.109375
- b_qkv: float32 [3, 2048], P(None, ('fsdp', 'head')), may hold values from -2.5 to 2.5
- qk_gain: float32 [2, 128], replicated, may hold values from 0.7 to 2.4
- block_lists: int32 [16, 27], P(('groups', 'seq')), parts along dimension 0, may hold values from -1 to 7, as said below
Outputs:
- attention: bfloat16 [6144, 2048], P(('groups', 'seq'), ('fsdp', 'head')), parts along dimension 0
There are 2 independent parts, one for each index of `groups`. A program takes and returns all parts, laid end to end along the dimension named above; an argument that names none is the same for every part. Nothing has to cross between parts.
Inputs may be any that keep to these rules, and one draw needn't show every extreme that they name: `block_lists`: tile g lies at width g // 2, time (g % 2) // 1 and height g % 1 of a 2 x 1 x 4 grid of tiles. Entry (a + 1) * 9 + (b + 1) * 3 + (c + 1) of row g, for a, b, c in -1, 0, 1, is the tile at time + a, height + b and width + c of tile g, or -1 where that tile is outside the grid or left out of the list. Entry 13 is always g.
All inputs are finite; a program needn't handle non-finite values.
Results may differ from a plain program's by a relative error of at most 0.0058.
Values may be sent and summed in bfloat16 or wider, within the bound.
No kernel may reach another device: no remote copies, remote signals or barrier semaphores. Data moves between devices by JAX's collectives and lax.ppermute only.
A program may use at most 128 MiB of HBM per device.

v0:
```python
import math
import jax
import jax.numpy as jnp
from jax import lax
from jax.sharding import PartitionSpec as P


def with_halo(shard, sides, width):
    for axis, dim in sides:
        devices, length = (lax.axis_size(axis), shard.shape[dim])
        up = [(i, (i + 1) % devices) for i in range(devices - 1)]
        down = [(j, i) for i, j in up]
        last = lax.slice_in_dim(shard, length - width, length, axis=dim)
        first = lax.slice_in_dim(shard, 0, width, axis=dim)
        before = lax.ppermute(last, axis, up)
        after = lax.ppermute(first, axis, down)
        shard = jnp.concatenate([before, shard, after], axis=dim)
    return shard


def normed_heads(tensor, gain_row, head_dim):
    shaped = tensor.reshape(tensor.shape[0], tensor.shape[1] // head_dim, head_dim)
    scaled = (
        shaped * lax.rsqrt(jnp.mean(shaped * shaped, axis=-1, keepdims=True) + 1e-06) * gain_row
    )
    return scaled.astype(jnp.bfloat16)


def reach_sides(key_rows, values):
    stacked = jnp.stack([key_rows, values], axis=0)
    return with_halo(stacked, (("seq", 1),), key_rows.shape[0])


def per_device(frames, modulation, w_qkv, b_qkv, qk_gain, block_lists):
    inputs = frames.astype(jnp.float32)
    average = jnp.mean(inputs, axis=-1, keepdims=True)
    centred = inputs - average
    variance = jnp.mean(centred * centred, axis=-1, keepdims=True)
    normed = centred * lax.rsqrt(variance + 1e-06) * (1.0 + modulation[0]) + modulation[1]
    normed = normed.astype(jnp.bfloat16)
    tokens = normed.shape[0]
    width_cols = w_qkv.shape[2]
    head_dim = qk_gain.shape[1]
    heads = width_cols // head_dim
    projected = jnp.einsum(
        "td,djc->tjc",
        normed,
        lax.all_gather(w_qkv, "seq", axis=0, tiled=True),
        preferred_element_type=jnp.float32,
    )
    projected = projected + b_qkv
    queries = normed_heads(projected[:, 0], qk_gain[0], head_dim)
    key_rows = normed_heads(projected[:, 1], qk_gain[1], head_dim)
    values = projected[:, 2].astype(jnp.bfloat16).reshape(tokens, heads, head_dim)
    neighbourhood = reach_sides(key_rows, values)
    position = lax.axis_index("seq")
    tile_dev = block_lists.shape[0]
    tile_len = tokens // tile_dev
    candidates = (position - 1) * tile_dev + jnp.arange(3 * tile_dev, dtype=jnp.int32)
    matches = (block_lists[:, :, None] == candidates[None, None, :]) & (
        block_lists[:, :, None] >= 0
    )
    allowed_tiles = jnp.any(matches, axis=1)
    allowed_keys = jnp.repeat(jnp.repeat(allowed_tiles, tile_len, axis=0), tile_len, axis=1)
    factor = 1.0 / math.sqrt(head_dim)
    scores = (
        jnp.einsum("qhd,khd->hqk", queries, neighbourhood[0], preferred_element_type=jnp.float32)
        * factor
    )
    weights = jnp.where(allowed_keys[None, :, :], jnp.exp(scores), 0.0)
    totals = jnp.sum(weights, axis=-1)
    mixture = jnp.einsum(
        "hqk,khd->qhd",
        weights.astype(jnp.bfloat16),
        neighbourhood[1],
        preferred_element_type=jnp.float32,
    )
    result = (mixture / jnp.transpose(totals)[:, :, None]).astype(jnp.bfloat16)
    return result.reshape(tokens, width_cols)


def solution(mesh):
    placed = (
        P(("groups", "seq"), None),
        P("groups", None),
        P("seq", None, ("fsdp", "head")),
        P(None, ("fsdp", "head")),
        P(),
        P(("groups", "seq"), None),
    )
    return jax.shard_map(
        per_device,
        mesh=mesh,
        in_specs=placed,
        out_specs=P(("groups", "seq"), ("fsdp", "head")),
        check_vma=False,
    )
```

profile of v0, /device:TPU:0, one launch (start us, length us, event | category | flops | bytes accessed | tf_op | source)
XLA Modules:
  0.0 278.2 jit_solution(9089081699902757114)
XLA Ops:
  6.5 0.0 copy-start.6
  6.5 0.0 all-gather.2.cloned.1.call-start
  6.5 4.3 %copy.27 = bf16[768,3,512]{0,2,1:T(8,128)(2,1)} copy(bf16[768,3,512]{2,0,1:T(8,128)(2,1)} %param.8) | data formatting | bytes 4718592 | tf_op args[2]
  10.8 0.0 all-gather.2.cloned.1.call-update
  10.9 0.0 copy-done.6
  10.9 0.0 copy-start
  10.9 0.0 copy-start.5
  10.9 0.0 copy-start.8
  10.9 3.2 %convert_reduce_fusion = f32[768]{0:T(1024)S(1)} fusion(bf16[768,3072]{1,0:T(8,128)(2,1)} %param.6), kind=kLoop, calls=%fused_computation.6 | loop fusion | flops 4717824 | bytes 4721664 | tf_op jit(solution)/shard_map/reduce_sum | solution.py:36
  14.1 0.5 copy-done
  14.6 1.4 fusion.7
  16.0 0.0 copy-done.5
  16.0 164.5 %all-gather.2.cloned.1.call-done = bf16[3072,3,512]{0,2,1:T(8,128)(2,1)} async-done(((bf16[768,3,512]{0,2,1:T(8,128)(2,1)}), bf16[3072,3,512]{0,2,1:T(8,128)(2,1)}) %all-gather.2.cloned.1.call-update) | async-done | bytes 9437200 | tf_op jit(solution)/shard_map/all_gather | solution.py:48
  180.5 0.0 copy-done.8
  180.5 11.9 %broadcast_add_fusion = f32[768,3,512]{0,2,1:T(8,128)S(1)} fusion(f32[3,512]{1,0:T(4,128)S(1)} %copy-done.8, bf16[3072,3,512]{0,2,1:T(8,128)(2,1)} %all-gather.2.cloned.1.call-done, bf16[768,3072]{1,0:T(8,128)(2,1)} %param.6, f32[3072]{0:T(1024)S(1)} %bitcast.43, f32[3072]{0:T(1024)S(1)} %bitcast.42, f32[768]{0:T(1024)S(1)} %add_rsqrt_fusion.2, ...), kind=kOutput, calls=%fused_computation.23 | convolution fusion | flops 7263092736 | bytes 18911232 | tf_op jit(solution)/shard_map/td,djc->tjc/dot_general | solution.py:45
  192.4 0.1 slice.53
  192.5 2.0 fusion.28
  194.5 0.4 copy.29
  194.9 1.5 reduce_sum.47
  196.4 0.0 copy-start.7
  196.4 3.0 %copy.28 = f32[1,768,4,128]{3,1,2,0:T(8,128)} copy(f32[1,768,4,128]{1,3,2,0:T(8,128)} %bitcast.37) | data formatting | bytes 3145728 | tf_op jit(solution)/shard_map/reshape;squeeze | solution.py:22
  199.5 1.9 multiply_convert_fusion.1
  201.4 1.3 pad_maximum_fusion.1
  202.6 1.3 collective-permute-start.1
  203.9 5.7 %collective-permute-start = (bf16[2,768,4,128]{3,1,2,0:T(8,128)(2,1)}, bf16[2,768,4,128]{3,1,2,0:T(8,128)(2,1)}, u32[]{:S(2)}, u32[]{:S(2)}) collective-permute-start(bf16[2,768,4,128]{3,1,2,0:T(8,128)(2,1)} %pad_maximum_fusion.1), channel_id=1, source_target_pairs={{0,4},{4,8},{8,12},{1,5},{5,9},{9,13},{2,6},{6,10},{10,14},{3,7},{... | collective-permute-start | bytes 4718600 | tf_op jit(solution)/shard_map/ppermute | solution.py:15
  209.7 0.0 copy-done.7
  209.7 0.2 and_reduce_fusion
  209.9 0.1 broadcast_in_dim.14
  209.9 1.7 broadcast_in_dim.19
  211.6 5.4 %copy.30 = pred[768,2304]{1,0:T(8,128)(4,1)} copy(pred[768,2304]{0,1:T(8,128)(4,1)} %bitcast.36) | data formatting | bytes 3538944 | tf_op jit(solution)/shard_map/jit(_where)/broadcast_in_dim | solution.py:70
  217.0 1.6 copy.31
  218.6 0.1 multiply_reduce_fusion
  218.8 0.0 copy-start.2
  218.8 0.0 copy-start.4
  218.8 22.4 %collective-permute-done.1 = bf16[2,768,4,128]{3,1,2,0:T(8,128)(2,1)} collective-permute-done((bf16[2,768,4,128]{3,1,2,0:T(8,128)(2,1)}, bf16[2,768,4,128]{3,1,2,0:T(8,128)(2,1)}, u32[]{:S(2)}, u32[]{:S(2)}) %collective-permute-start.1) | collective-permute-done | bytes 1572896 | tf_op jit(solution)/shard_map/ppermute | solution.py:16
  241.2 1.2 collective-permute-done
  242.4 2.0 pad_maximum_fusion
  244.4 0.0 copy-start.1
  244.4 0.0 copy-done.2
  244.4 0.0 copy-done.4
  244.4 0.0 copy-start.3
  244.4 12.9 %fusion = (f32[4,768]{1,0:T(4,128)S(1)}, f32[4,768,2304]{2,1,0:T(8,128)}) fusion(pred[768,2304]{1,0:T(8,128)(4,1)S(1)} %copy-done.2, bf16[2,2304,4,128]{3,1,2,0:T(8,128)(2,1)S(1)} %pad_maximum_fusion, f32[768,4,128]{2,0,1:T(8,128)S(1)} %copy-done.4, f32[128]{0:T(128)S(1)} %get-tuple-element.10, f32[768,4]{0,1:T(4,128)S(1)} %add_rsqrt_fusion), kind=kOutput, calls=%fused_computation.1 | convolution fusion | flops 1834349568 | bytes 34038272 | tf_op jit(solution)/shard_map/qhd,khd->hqk/dot_general | solution.py:67
  257.3 0.0 copy-done.1
  257.3 0.0 copy-done.3
  257.3 12.9 %fusion.21 = bf16[768,4,128]{0,2,1:T(8,128)(2,1)S(1)} fusion(f32[768,4]{0,1:T(4,128)S(1)} %bitcast.44, f32[4,768,2304]{2,1,0:T(8,128)} %get-tuple-element.13, pred[768,2304]{1,0:T(8,128)(4,1)S(1)} %copy-done.3, bf16[2,2304,4,128]{3,1,2,0:T(8,128)(2,1)} %copy-done.1), kind=kOutput, calls=%fused_computation.27 | convolution fusion | flops 1833959424 | bytes 33239040 | tf_op jit(solution)/shard_map/hqk,khd->qhd/dot_general | solution.py:72
  270.2 1.2 copy.33
  (8 shorter events, 0.1 us)
Async XLA Ops:
  6.5 4.3 %copy-start.6 = (f32[2,128]{1,0:T(2,128)S(1)}, f32[2,128]{1,0:T(2,128)}, u32[]{:S(2)}) copy-start(f32[2,128]{1,0:T(2,128)} %param.10) | copy-start | bytes 3076
  6.5 174.0 %all-gather.2.cloned.1.call-start = ((), (), s32[]{:S(2)}) async-start(), calls=%async_computation | async-start | bytes 11796480 | tf_op jit(solution)/shard_map/all_gather | solution.py:48
  10.9 3.8 %copy-start = (bf16[768,3072]{1,0:T(8,128)(2,1)S(1)}, bf16[768,3072]{1,0:T(8,128)(2,1)}, u32[]{:S(2)}) copy-start(bf16[768,3072]{1,0:T(8,128)(2,1)} %param.6) | copy-start | bytes 14155780
  10.9 5.1 %copy-start.5 = (f32[2,3072]{1,0:T(2,128)S(1)}, f32[2,3072]{1,0:T(2,128)}, u32[]{:S(2)}) copy-start(f32[2,3072]{1,0:T(2,128)} %param.7) | copy-start | bytes 73732
  10.9 169.6 %copy-start.8 = (f32[3,512]{1,0:T(4,128)S(1)}, f32[3,512]{1,0:T(4,128)}, u32[]{:S(2)}) copy-start(f32[3,512]{1,0:T(4,128)} %param.9) | copy-start | bytes 18436
  196.4 13.3 %copy-start.7 = (s32[2,27]{1,0:T(2,128)S(1)}, s32[2,27]{1,0:T(2,128)}, u32[]{:S(2)}) copy-start(s32[2,27]{1,0:T(2,128)} %param.11) | copy-start | bytes 652
  202.6 38.6 %collective-permute-start.1 = (bf16[2,768,4,128]{3,1,2,0:T(8,128)(2,1)}, bf16[2,768,4,128]{3,1,2,0:T(8,128)(2,1)}, u32[]{:S(2)}, u32[]{:S(2)}) collective-permute-start(bf16[2,768,4,128]{3,1,2,0:T(8,128)(2,1)} %pad_maximum_fusion.1), channel_id=1, source_target_pairs={{4,0},{8,4},{12,8},{5,1},{9,5},{13,9},{6,2},{10,6},{14,10},{7,3},{... | collective-permute-start | bytes 4718600 | tf_op jit(solution)/shard_map/ppermute | solution.py:16
  203.9 38.4 %collective-permute-start = (bf16[2,768,4,128]{3,1,2,0:T(8,128)(2,1)}, bf16[2,768,4,128]{3,1,2,0:T(8,128)(2,1)}, u32[]{:S(2)}, u32[]{:S(2)}) collective-permute-start(bf16[2,768,4,128]{3,1,2,0:T(8,128)(2,1)} %pad_maximum_fusion.1), channel_id=1, source_target_pairs={{0,4},{4,8},{8,12},{1,5},{5,9},{9,13},{2,6},{6,10},{10,14},{3,7},{... | collective-permute-start | bytes 4718600 | tf_op jit(solution)/shard_map/ppermute | solution.py:15
  218.8 25.6 %copy-start.2 = (pred[768,2304]{1,0:T(8,128)(4,1)S(1)}, pred[768,2304]{1,0:T(8,128)(4,1)}, u32[]{:S(2)}) copy-start(pred[768,2304]{1,0:T(8,128)(4,1)} %copy.30) | copy-start | bytes 5308420
  218.8 25.6 %copy-start.4 = (f32[768,4,128]{2,0,1:T(8,128)S(1)}, f32[768,4,128]{2,0,1:T(8,128)}, u32[]{:S(2)}) copy-start(f32[768,4,128]{2,0,1:T(8,128)} %copy.31) | copy-start | bytes 4718596
  244.4 12.9 %copy-start.1 = (bf16[2,2304,4,128]{3,1,2,0:T(8,128)(2,1)}, bf16[2,2304,4,128]{3,1,2,0:T(8,128)(2,1)S(1)}, u32[]{:S(2)}) copy-start(bf16[2,2304,4,128]{3,1,2,0:T(8,128)(2,1)S(1)} %pad_maximum_fusion) | copy-start | bytes 14155780
  244.4 12.9 %copy-start.3 = (pred[768,2304]{1,0:T(8,128)(4,1)S(1)}, pred[768,2304]{1,0:T(8,128)(4,1)}, u32[]{:S(2)}) copy-start(pred[768,2304]{1,0:T(8,128)(4,1)} %copy.30) | copy-start | bytes 5308420
Sparse Core Ops, SparseCore 0:
  11.0 169.4 all-gather.1
where the time goes:
time: 279 us; the launch traced here: 278 us
  waiting for transfers between devices  188 us (67%)
  matrix products  37.7 us (14%)
  local copies, waits for them, and re-layouts  18.3 us (7%)
  other arithmetic  13.7 us (5%)
  between operations  13.6 us (5%)
  starting transfers between devices  7 us (3%)
    all_gather x1, waiting for transfers between devices, per_device(): lax.all_gather(w_qkv, 'seq', axis=0, tiled=True)  164 us
    ppermute x1, waiting for transfers between devices, with_halo(): after = lax.ppermute(first, axis, down)  22.4 us
    dot_general x1, matrix products, per_device(): jnp.einsum('qhd,khd->hqk', queries, neighbourhood[0], preferred_element_t...  12.9 us
    dot_general x1, matrix products, per_device(): jnp.einsum('hqk,khd->qhd', weights.astype(jnp.bfloat16), neighbourhood[1]...  12.9 us
    dot_general x1, matrix products, per_device(): jnp.einsum('td,djc->tjc', normed, lax.all_gather(w_qkv, 'seq', axis=0, ti...  11.9 us
    ppermute x1, starting transfers between devices, with_halo(): before = lax.ppermute(last, axis, up)  5.72 us
  transfers between devices with their start and end apart: 3, of which 3 were waited for; matrix products, arithmetic and copies ran while one was open for 5% of the time, Pallas kernels for 0%

commit v1 on v0

--- a/solution.py
+++ b/solution.py
@@ -3,6 +3,18 @@
 import jax.numpy as jnp
 from jax import lax
 from jax.sharding import PartitionSpec as P
+
+
+def ring_product(array, axis, dim, term):
+    count, index, extent = (lax.axis_size(axis), lax.axis_index(axis), array.shape[dim])
+    upward = [(i, (i + 1) % count) for i in range(count)]
+    held, subtotal = (array, None)
+    for step in range(count):
+        following = lax.ppermute(held, axis, upward) if step < count - 1 else None
+        absorb = term(held, (index - step) % count * extent)
+        subtotal = absorb if subtotal is None else subtotal + absorb
+        held = following
+    return subtotal
 
 
 def with_halo(shard, sides, width):
@@ -42,11 +54,16 @@
     width_cols = w_qkv.shape[2]
     head_dim = qk_gain.shape[1]
     heads = width_cols // head_dim
-    projected = jnp.einsum(
-        "td,djc->tjc",
-        normed,
-        lax.all_gather(w_qkv, "seq", axis=0, tiled=True),
-        preferred_element_type=jnp.float32,
+    projected = ring_product(
+        w_qkv,
+        "seq",
+        0,
+        lambda shard_2, start: jnp.einsum(
+            "td,djc->tjc",
+            lax.dynamic_slice_in_dim(normed, start, shard_2.shape[0], axis=1),
+            shard_2,
+            preferred_element_type=jnp.float32,
+        ),
     )
     projected = projected + b_qkv
     queries = normed_heads(projected[:, 0], qk_gain[0], head_dim)

time: 279 us -> 246 us (0.88)
  waiting for transfers between devices: 188 us -> 164 us
  between operations: 13.6 us -> 0.37 us
  other arithmetic: 13.7 us -> 19.7 us
  starting transfers between devices: 7 us -> 10.1 us
    all_gather x1 -> x0, waiting for transfers between devices: 164 us -> none  [per_device(): lax.all_gather(w_qkv, 'seq', axis=0, tiled=True)]
    ppermute x0 -> x3, waiting for transfers between devices: none -> 143 us  [ring_product(): following = lax.ppermute(held, axis, upward) if step < count - 1 else None]
    convert_element_type x0 -> x1, other arithmetic: none -> 5.13 us  [per_device(): normed = normed.astype(jnp.bfloat16)]
    ppermute x0 -> x3, starting transfers between devices: none -> 3.08 us  [ring_product(): following = lax.ppermute(held, axis, upward) if step < count - 1 else None]
    dot_general x1 -> x4, matrix products: 11.9 us -> 10.1 us  [per_device(): jnp.einsum('td,djc->tjc', lax.dynamic_slice_in_dim(normed, start, shard_2...]
  transfers between devices with their start and end apart: 3 -> 5, of which waited for: 3 -> 5; matrix products, arithmetic and copies ran while one was open for 5% -> 11% of each run, Pallas kernels for 0% -> 0%
where the time goes in v1:
time: 246 us
  waiting for transfers between devices  164 us (67%)
  matrix products  35.8 us (15%)
  other arithmetic  19.7 us (8%)
  local copies, waits for them, and re-layouts  16.3 us (7%)
  starting transfers between devices  10.1 us (4%)
    ppermute x3, waiting for transfers between devices, ring_product(): following = lax.ppermute(held, axis, upward) if step < count - 1 else None  143 us
    ppermute x1, waiting for transfers between devices, with_halo(): after = lax.ppermute(first, axis, down)  19.7 us
    dot_general x1, matrix products, per_device(): jnp.einsum('hqk,khd->qhd', weights.astype(jnp.bfloat16), neighbourhood[1]...  12.9 us
    dot_general x1, matrix products, per_device(): jnp.einsum('qhd,khd->hqk', queries, neighbourhood[0], preferred_element_t...  12.8 us
    dot_general x4, matrix products, per_device(): jnp.einsum('td,djc->tjc', lax.dynamic_slice_in_dim(normed, start, shard_2...  10.1 us
    ppermute x1, starting transfers between devices, with_halo(): before = lax.ppermute(last, axis, up)  5.74 us
    broadcast_in_dim x1, local copies, waits for them, and re-layouts, per_device(): weights = jnp.where(allowed_keys[None, :, :], jnp.exp(scores), 0.0)  5.38 us
    convert_element_type x1, other arithmetic, per_device(): normed = normed.astype(jnp.bfloat16)  5.13 us
  transfers between devices with their start and end apart: 5, of which 5 were waited for; matrix products, arithmetic and copies ran while one was open for 11% of the time, Pallas kernels for 0%

profile of v1, /device:TPU:0, one launch (start us, length us, event | category | flops | bytes accessed | tf_op | source)
XLA Modules:
  0.0 245.9 jit_solution(13595194201801755748)
XLA Ops:
  0.0 2.8 %copy.31 = bf16[768,3,512]{0,2,1:T(8,128)(2,1)S(1)} copy(bf16[768,3,512]{2,0,1:T(8,128)(2,1)} %param.8) | data formatting | bytes 4718592 | tf_op args[2]
  2.8 0.0 copy-start
  2.9 0.0 copy-start.7
  2.9 0.0 copy-start.8
  2.9 3.1 %collective-permute-start = (bf16[768,3,512]{0,2,1:T(8,128)(2,1)S(1)}, bf16[768,3,512]{0,2,1:T(8,128)(2,1)S(1)}, u32[]{:S(2)}, u32[]{:S(2)}) collective-permute-start(bf16[768,3,512]{0,2,1:T(8,128)(2,1)S(1)} %copy.31), channel_id=1, source_target_pairs={{0,4},{4,8},{8,12},{12,0},{1,5},{5,9},{9,13},{13,1},{2,6},{6,10},{... | collective-permute-start | bytes 7077896 | tf_op jit(solution)/shard_map/ppermute | solution.py:13
  6.0 53.3 %collective-permute-done = bf16[768,3,512]{0,2,1:T(8,128)(2,1)S(1)} collective-permute-done((bf16[768,3,512]{0,2,1:T(8,128)(2,1)S(1)}, bf16[768,3,512]{0,2,1:T(8,128)(2,1)S(1)}, u32[]{:S(2)}, u32[]{:S(2)}) %collective-permute-start) | collective-permute-done | bytes 2359328 | tf_op jit(solution)/shard_map/ppermute | solution.py:13
  59.2 0.0 copy-start.10
  59.2 0.0 collective-permute-start.1
  59.2 3.9 %convert_reduce_fusion = f32[768]{0:T(1024)S(1)} fusion(bf16[768,3072]{1,0:T(8,128)(2,1)} %param.6), kind=kLoop, calls=%fused_computation.6 | loop fusion | flops 4717824 | bytes 4721664 | tf_op jit(solution)/shard_map/reduce_sum | solution.py:48
  63.1 0.0 copy-done
  63.1 1.4 fusion.7
  64.5 0.0 copy-done.10
  64.5 0.0 copy-done.7
  64.5 49.0 %collective-permute-done.1 = bf16[768,3,512]{0,2,1:T(8,128)(2,1)} collective-permute-done((bf16[768,3,512]{0,2,1:T(8,128)(2,1)S(1)}, bf16[768,3,512]{0,2,1:T(8,128)(2,1)}, u32[]{:S(2)}, u32[]{:S(2)}) %collective-permute-start.1) | collective-permute-done | bytes 2359328 | tf_op jit(solution)/shard_map/ppermute | solution.py:13
  113.6 0.0 collective-permute-start.2
  113.6 0.0 copy-done.8
  113.7 0.0 copy-start.2
  113.7 5.1 %fusion.10 = bf16[768,3072]{1,0:T(8,128)(2,1)S(1)} fusion(bf16[768,3072]{1,0:T(8,128)(2,1)} %param.6, f32[3072]{0:T(1024)S(1)} %bitcast.52, f32[3072]{0:T(1024)S(1)} %bitcast.51, f32[768]{0:T(1024)S(1)} %add_rsqrt_fusion.2, f32[768]{0:T(1024)S(1)} %broadcast_multiply_fusion), kind=kLoop, calls=%fused_computation.12 | loop fusion | flops 14155776 | bytes 9467904 | tf_op jit(solution)/shard_map/convert_element_type | solution.py:52
  118.8 0.0 copy-done.2
  118.8 0.0 copy-start.11
  118.8 2.0 fusion.18
  120.9 0.0 copy-done.11
  120.9 2.1 fusion.16
  123.0 0.0 copy-start.6
  123.0 3.7 %fusion.14 = f32[768,3,512]{0,2,1:T(8,128)S(1)} fusion(bf16[768,3,512]{0,2,1:T(8,128)(2,1)} %collective-permute-done.1, bf16[768,3072]{1,0:T(8,128)(2,1)S(1)} %fusion.10, s32[]{:T(128)S(6)} %select_n.40), kind=kOutput, calls=%fused_computation.26 | convolution fusion | flops 1811939328 | bytes 8257540 | tf_op jit(solution)/shard_map/td,djc->tjc/dot_general | solution.py:61
  126.7 40.4 %collective-permute-done.2 = bf16[768,3,512]{0,2,1:T(8,128)(2,1)S(1)} collective-permute-done((bf16[768,3,512]{0,2,1:T(8,128)(2,1)}, bf16[768,3,512]{0,2,1:T(8,128)(2,1)S(1)}, u32[]{:S(2)}, u32[]{:S(2)}) %collective-permute-start.2) | collective-permute-done | bytes 2359328 | tf_op jit(solution)/shard_map/ppermute | solution.py:13
  167.1 0.0 copy-done.6
  167.1 2.3 add_add_fusion
  169.4 0.1 slice.53
  169.5 2.0 fusion.34
  171.5 0.4 copy.33
  171.9 1.5 reduce_sum.47
  173.4 0.0 copy-start.9
  173.4 3.0 %copy.32 = f32[1,768,4,128]{3,1,2,0:T(8,128)} copy(f32[1,768,4,128]{1,3,2,0:T(8,128)} %bitcast.47) | data formatting | bytes 3145728 | tf_op jit(solution)/shard_map/reshape;squeeze | solution.py:34
  176.5 1.9 multiply_convert_fusion.1
  178.3 1.5 pad_maximum_fusion.1
  179.8 1.3 collective-permute-start.4
  181.1 5.7 %collective-permute-start.3 = (bf16[2,768,4,128]{3,1,2,0:T(8,128)(2,1)}, bf16[2,768,4,128]{3,1,2,0:T(8,128)(2,1)}, u32[]{:S(2)}, u32[]{:S(2)}) collective-permute-start(bf16[2,768,4,128]{3,1,2,0:T(8,128)(2,1)} %pad_maximum_fusion.1), channel_id=1, source_target_pairs={{0,4},{4,8},{8,12},{1,5},{5,9},{9,13},{2,6},{6,10},{10,14},{3,7},{... | collective-permute-start | bytes 4718600 | tf_op jit(solution)/shard_map/ppermute | solution.py:27
  186.9 0.0 copy-done.9
  186.9 0.2 and_reduce_fusion
  187.1 0.1 broadcast_in_dim.14
  187.1 1.7 broadcast_in_dim.19
  188.8 5.4 %copy.34 = pred[768,2304]{1,0:T(8,128)(4,1)} copy(pred[768,2304]{0,1:T(8,128)(4,1)} %bitcast.46) | data formatting | bytes 3538944 | tf_op jit(solution)/shard_map/jit(_where)/broadcast_in_dim | solution.py:87
  194.2 1.6 copy.35
  195.9 0.1 multiply_reduce_fusion
  196.0 0.0 copy-start.3
  196.0 0.0 copy-start.5
  196.0 19.7 %collective-permute-done.4 = bf16[2,768,4,128]{3,1,2,0:T(8,128)(2,1)} collective-permute-done((bf16[2,768,4,128]{3,1,2,0:T(8,128)(2,1)}, bf16[2,768,4,128]{3,1,2,0:T(8,128)(2,1)}, u32[]{:S(2)}, u32[]{:S(2)}) %collective-permute-start.4) | collective-permute-done | bytes 1572896 | tf_op jit(solution)/shard_map/ppermute | solution.py:28
  215.8 1.2 collective-permute-done.3
  217.0 2.0 pad_maximum_fusion
  219.0 0.0 copy-start.1
  219.0 0.0 copy-done.3
  219.0 0.0 copy-done.5
  219.0 0.0 copy-start.4
  219.0 12.8 %fusion = (f32[4,768]{1,0:T(4,128)S(1)}, f32[4,768,2304]{2,1,0:T(8,128)}) fusion(pred[768,2304]{1,0:T(8,128)(4,1)S(1)} %copy-done.3, bf16[2,2304,4,128]{3,1,2,0:T(8,128)(2,1)S(1)} %pad_maximum_fusion, f32[768,4,128]{2,0,1:T(8,128)S(1)} %copy-done.5, f32[128]{0:T(128)S(1)} %get-tuple-element.10, f32[768,4]{0,1:T(4,128)S(1)} %add_rsqrt_fusion), kind=kOutput, calls=%fused_computation.1 | convolution fusion | flops 1834349568 | bytes 34038272 | tf_op jit(solution)/shard_map/qhd,khd->hqk/dot_general | solution.py:84
  231.9 0.0 copy-done.1
  231.9 0.0 copy-done.4
  231.9 12.9 %fusion.12 = bf16[768,4,128]{0,2,1:T(8,128)(2,1)S(1)} fusion(f32[768,4]{0,1:T(4,128)S(1)} %bitcast.54, f32[4,768,2304]{2,1,0:T(8,128)} %get-tuple-element.13, pred[768,2304]{1,0:T(8,128)(4,1)S(1)} %copy-done.4, bf16[2,2304,4,128]{3,1,2,0:T(8,128)(2,1)} %copy-done.1), kind=kOutput, calls=%fused_computation.21 | convolution fusion | flops 1833959424 | bytes 33239040 | tf_op jit(solution)/shard_map/hqk,khd->qhd/dot_general | solution.py:89
  244.7 1.2 copy.37
  (8 shorter events, 0.1 us)
Async XLA Ops:
  2.8 60.3 %copy-start = (bf16[768,3072]{1,0:T(8,128)(2,1)S(1)}, bf16[768,3072]{1,0:T(8,128)(2,1)}, u32[]{:S(2)}) copy-start(bf16[768,3072]{1,0:T(8,128)(2,1)} %param.6) | copy-start | bytes 14155780
  2.9 61.7 %copy-start.7 = (f32[2,3072]{1,0:T(2,128)S(1)}, f32[2,3072]{1,0:T(2,128)}, u32[]{:S(2)}) copy-start(f32[2,3072]{1,0:T(2,128)} %param.7) | copy-start | bytes 73732
  2.9 110.7 %copy-start.8 = (f32[2,128]{1,0:T(2,128)S(1)}, f32[2,128]{1,0:T(2,128)}, u32[]{:S(2)}) copy-start(f32[2,128]{1,0:T(2,128)} %param.10) | copy-start | bytes 3076
  2.9 56.3 %collective-permute-start = (bf16[768,3,512]{0,2,1:T(8,128)(2,1)S(1)}, bf16[768,3,512]{0,2,1:T(8,128)(2,1)S(1)}, u32[]{:S(2)}, u32[]{:S(2)}) collective-permute-start(bf16[768,3,512]{0,2,1:T(8,128)(2,1)S(1)} %copy.31), channel_id=1, source_target_pairs={{0,4},{4,8},{8,12},{12,0},{1,5},{5,9},{9,13},{13,1},{2,6},{6,10},{... | collective-permute-start | bytes 7077896 | tf_op jit(solution)/shard_map/ppermute | solution.py:13
  59.2 5.3 %copy-start.10 = (bf16[768,3,512]{0,2,1:T(8,128)(2,1)}, bf16[768,3,512]{0,2,1:T(8,128)(2,1)S(1)}, u32[]{:S(2)}) copy-start(bf16[768,3,512]{0,2,1:T(8,128)(2,1)S(1)} %collective-permute-done) | copy-start | bytes 7077892
  59.2 54.3 %collective-permute-start.1 = (bf16[768,3,512]{0,2,1:T(8,128)(2,1)S(1)}, bf16[768,3,512]{0,2,1:T(8,128)(2,1)}, u32[]{:S(2)}, u32[]{:S(2)}) collective-permute-start(bf16[768,3,512]{0,2,1:T(8,128)(2,1)S(1)} %collective-permute-done), channel_id=1, source_target_pairs={{0,4},{4,8},{8,12},{12,0},{1,5},{5,9},{9,13},{13,1},{2,6},{6,10},{... | collective-permute-start | bytes 7077896 | tf_op jit(solution)/shard_map/ppermute | solution.py:13
  113.6 53.5 %collective-permute-start.2 = (bf16[768,3,512]{0,2,1:T(8,128)(2,1)}, bf16[768,3,512]{0,2,1:T(8,128)(2,1)S(1)}, u32[]{:S(2)}, u32[]{:S(2)}) collective-permute-start(bf16[768,3,512]{0,2,1:T(8,128)(2,1)} %collective-permute-done.1), channel_id=1, source_target_pairs={{0,4},{4,8},{8,12},{12,0},{1,5},{5,9},{9,13},{13,1},{2,6},{6,10},{... | collective-permute-start | bytes 7077896 | tf_op jit(solution)/shard_map/ppermute | solution.py:13
  113.7 5.2 %copy-start.2 = (bf16[768,3,512]{2,0,1:T(8,128)(2,1)S(1)}, bf16[768,3,512]{2,0,1:T(8,128)(2,1)}, u32[]{:S(2)}) copy-start(bf16[768,3,512]{2,0,1:T(8,128)(2,1)} %param.8) | copy-start | bytes 7077892
  118.8 2.1 copy-start.11
  123.0 44.1 %copy-start.6 = (f32[3,512]{1,0:T(4,128)S(1)}, f32[3,512]{1,0:T(4,128)}, u32[]{:S(2)}) copy-start(f32[3,512]{1,0:T(4,128)} %param.9) | copy-start | bytes 18436
  173.4 13.5 %copy-start.9 = (s32[2,27]{1,0:T(2,128)S(1)}, s32[2,27]{1,0:T(2,128)}, u32[]{:S(2)}) copy-start(s32[2,27]{1,0:T(2,128)} %param.11) | copy-start | bytes 652
  179.8 35.9 %collective-permute-start.4 = (bf16[2,768,4,128]{3,1,2,0:T(8,128)(2,1)}, bf16[2,768,4,128]{3,1,2,0:T(8,128)(2,1)}, u32[]{:S(2)}, u32[]{:S(2)}) collective-permute-start(bf16[2,768,4,128]{3,1,2,0:T(8,128)(2,1)} %pad_maximum_fusion.1), channel_id=1, source_target_pairs={{4,0},{8,4},{12,8},{5,1},{9,5},{13,9},{6,2},{10,6},{14,10},{7,3},{... | collective-permute-start | bytes 4718600 | tf_op jit(solution)/shard_map/ppermute | solution.py:28
  181.1 35.8 %collective-permute-start.3 = (bf16[2,768,4,128]{3,1,2,0:T(8,128)(2,1)}, bf16[2,768,4,128]{3,1,2,0:T(8,128)(2,1)}, u32[]{:S(2)}, u32[]{:S(2)}) collective-permute-start(bf16[2,768,4,128]{3,1,2,0:T(8,128)(2,1)} %pad_maximum_fusion.1), channel_id=1, source_target_pairs={{0,4},{4,8},{8,12},{1,5},{5,9},{9,13},{2,6},{6,10},{10,14},{3,7},{... | collective-permute-start | bytes 4718600 | tf_op jit(solution)/shard_map/ppermute | solution.py:27
  196.0 23.0 %copy-start.3 = (pred[768,2304]{1,0:T(8,128)(4,1)S(1)}, pred[768,2304]{1,0:T(8,128)(4,1)}, u32[]{:S(2)}) copy-start(pred[768,2304]{1,0:T(8,128)(4,1)} %copy.34) | copy-start | bytes 5308420
  196.0 23.0 %copy-start.5 = (f32[768,4,128]{2,0,1:T(8,128)S(1)}, f32[768,4,128]{2,0,1:T(8,128)}, u32[]{:S(2)}) copy-start(f32[768,4,128]{2,0,1:T(8,128)} %copy.35) | copy-start | bytes 4718596
  219.0 12.9 %copy-start.1 = (bf16[2,2304,4,128]{3,1,2,0:T(8,128)(2,1)}, bf16[2,2304,4,128]{3,1,2,0:T(8,128)(2,1)S(1)}, u32[]{:S(2)}) copy-start(bf16[2,2304,4,128]{3,1,2,0:T(8,128)(2,1)S(1)} %pad_maximum_fusion) | copy-start | bytes 14155780
  219.0 12.9 %copy-start.4 = (pred[768,2304]{1,0:T(8,128)(4,1)S(1)}, pred[768,2304]{1,0:T(8,128)(4,1)}, u32[]{:S(2)}) copy-start(pred[768,2304]{1,0:T(8,128)(4,1)} %copy.34) | copy-start | bytes 5308420
